TPU v7x, 32 devices: a whole 2x2x4 slice. The times are simulated.
32 devices in a mesh: rep: 8 (over z, core), mdl: 4 (over y, x).
Axes of the slice: x: 2, y: 2, z: 4, core: 2. Of those that a mesh axis runs over, the one named last changes fastest.
Arguments:
- deltas: bfloat16 [8, 2560, 2560], P('rep', 'mdl'), may hold values from -72 to 72
- errors: bfloat16 [8, 2560, 2560], P('rep', 'mdl'), may hold values from -3 to 3
- starts: float32 [2560, 64], replicated, may hold values from -6 to 6
- momentum: float32 [2560, 2560], P('mdl', 'rep'), may hold values from -2 to 2
Outputs:
- new_errors: bfloat16 [8, 2560, 2560], P('rep', 'mdl')
- new_momentum: float32 [2560, 2560], P('mdl', 'rep')
- outer_step: float32 [2560, 2560], P('mdl', 'rep')
All inputs are finite; a program needn't handle non-finite values.
Results may differ from a plain program's by a relative error of at most 0.001.
Values sent between devices are 32-bit elements; how exact they have to be, the bound alone decides.
A program may use at most 64 MiB of HBM per device.

v0:
```python
import jax
import jax.numpy as jnp
from jax import lax
from jax.sharding import PartitionSpec as P

highest = lax.Precision.HIGHEST


def body(deltas, errors, starts, momentum):
    replicas = lax.axis_size("rep")
    merged = deltas[0].astype(jnp.float32) + errors[0].astype(jnp.float32)
    left_part = jnp.einsum("ac,ck->ka", merged, starts, precision=highest)
    left = lax.psum(left_part, "rep") / replicas
    gram = jnp.einsum("ka,la->kl", left, left, precision=highest)
    gram = lax.psum(gram, "mdl")
    lower = jnp.linalg.cholesky(gram)
    basis = jax.scipy.linalg.solve_triangular(lower, left, lower=True)
    right_part = jnp.einsum("ac,ka->kc", merged, basis, precision=highest)
    column_shares = lax.psum_scatter(right_part, "mdl", scatter_dimension=1, tiled=True)
    column_shares = lax.psum(column_shares, "rep")
    right = lax.all_gather(column_shares, "mdl", axis=1, tiled=True) / replicas
    approx = jnp.einsum("ka,kc->ac", basis, right, precision=highest)
    new_errors = (merged - approx).astype(jnp.bfloat16)[None]
    width = momentum.shape[1]
    owned = lax.dynamic_slice_in_dim(approx, lax.axis_index("rep") * width, width, 1)
    new_momentum = 0.9 * momentum + owned
    outer_step = 0.7 * (owned + 0.9 * new_momentum)
    return (new_errors, new_momentum, outer_step)


def solution(mesh):
    placed = (P("rep", "mdl", None), P("rep", "mdl", None), P(), P("mdl", "rep"))
    return jax.shard_map(
        body,
        mesh=mesh,
        in_specs=placed,
        out_specs=(P("rep", "mdl", None), P("mdl", "rep"), P("mdl", "rep")),
        check_vma=False,
    )
```

profile of v0, /device:TPU:0, one launch (start us, length us, event | category | flops | bytes accessed | tf_op | source)
XLA Modules:
  0.0 226.7 jit_solution(16170956885530419653)
XLA Ops:
  7.2 0.0 copy-start
  7.2 0.0 copy-start.3
  7.2 0.0 all-reduce.3.cloned.1.call-start
  7.2 1.0 copy-done
  8.3 9.4 %fusion.6 = f32[64,640]{1,0:T(8,128)} fusion(f32[2560,64]{0,1:T(8,128)S(1)} %copy-done, bf16[1,640,2560]{2,1,0:T(8,128)(2,1)} %param.5, bf16[1,640,2560]{2,1,0:T(8,128)(2,1)} %param.4), kind=kOutput, calls=%fused_computation.8 | convolution fusion | flops 1263206400 | bytes 7372800 | tf_op jit(solution)/shard_map/ac,ck->ka/dot_general | solution.py:12
  17.6 0.0 all-reduce.3.cloned.1.call-update
  17.7 0.0 reduce-scatter.2.cloned.1.call-start
  17.7 55.5 %all-reduce.3.cloned.1.call-done = f32[64,640]{1,0:T(8,128)} async-done(((f32[64,640]{1,0:T(8,128)}), f32[64,640]{1,0:T(8,128)}) %all-reduce.3.cloned.1.call-update) | async-done | bytes 163856 | tf_op jit(solution)/shard_map/psum | solution.py:13
  73.2 1.3 fusion.14
  74.5 16.2 %psum.22 = f32[64,64]{0,1:T(8,128)S(1)} all-reduce(f32[64,64]{0,1:T(8,128)S(1)} %fusion.14), channel_id=1, replica_groups=mesh['rep'=8,'mdl'=4] {'mdl'}, use_global_device_ids=true, to_apply=%region_1.0 | all-reduce | flops 4096 | bytes 32768 | tf_op jit(solution)/shard_map/psum | solution.py:15
  90.7 0.1 copy.8
  90.8 5.8 %cholesky.16 = f32[64,64]{1,0:T(8,128)S(1)} custom-call(f32[64,64]{1,0:T(8,128)S(1)} %fusion.20), custom_call_target="Cholesky" | custom-call | tf_op jit(solution)/shard_map/jit(cholesky)/cholesky | solution.py:16
  96.7 0.6 compare_reduce_fusion
  97.3 0.7 fusion.18
  98.0 4.9 %custom-call.7 = f32[1,64,64]{1,2,0:T(8,128)S(1)} custom-call(f32[1,64,64]{2,1,0:T(8,128)S(1)} %fusion.18), custom_call_target="InvertDiagBlocksLowerTriangular" | custom-call | tf_op jit(solution)/shard_map/jit(_solve_triangular)/triangular_solve | solution.py:17
  102.9 1.3 fusion.12
  104.2 8.3 %fusion = f32[64,2560]{1,0:T(8,128)} fusion(f32[64,640]{1,0:T(8,128)S(1)} %fusion.12, bf16[1,640,2560]{2,1,0:T(8,128)(2,1)} %param.5, bf16[1,640,2560]{2,1,0:T(8,128)(2,1)} %param.4), kind=kOutput, calls=%fused_computation.1 | convolution fusion | flops 1263206400 | bytes 7372800 | tf_op jit(solution)/shard_map/ac,ka->kc/dot_general | solution.py:18
  112.5 0.0 reduce-scatter.2.cloned.1.call-update
  112.5 0.0 all-reduce.5.cloned.1.call-start
  112.6 25.6 %reduce-scatter.2.cloned.1.call-done = f32[64,640]{1,0:T(8,128)} async-done(((f32[64,2560]{1,0:T(8,128)}), f32[64,640]{1,0:T(8,128)}) %reduce-scatter.2.cloned.1.call-update) | async-done | bytes 163856 | tf_op jit(solution)/shard_map/reduce_scatter | solution.py:19
  138.2 0.0 all-reduce.5.cloned.1.call-update
  138.3 0.0 copy-done.3
  138.3 0.3 copy.9
  138.6 54.7 %all-reduce.5.cloned.1.call-done = f32[64,640]{1,0:T(8,128)} async-done(((f32[64,640]{1,0:T(8,128)}), f32[64,640]{1,0:T(8,128)}) %all-reduce.5.cloned.1.call-update) | async-done | bytes 163856 | tf_op jit(solution)/shard_map/psum | solution.py:20
  193.3 13.2 %all_gather.3 = f32[64,2560]{1,0:T(8,128)S(1)} all-gather(f32[64,640]{1,0:T(8,128)} %all-reduce.5.cloned.1.call-done), channel_id=1, replica_groups=mesh['rep'=8,'mdl'=4] {'mdl'}, dimensions={1}, use_global_device_ids=true | all-gather | bytes 819200 | tf_op jit(solution)/shard_map/all_gather | solution.py:21
  206.4 5.4 %fusion.9 = f32[640,2560]{1,0:T(8,128)S(1)} fusion(f32[64,640]{1,0:T(8,128)S(1)} %fusion.12, f32[64,2560]{1,0:T(8,128)S(1)} %all_gather.3), kind=kOutput, calls=%fused_computation.11 | convolution fusion | flops 1258455040 | bytes 7372800 | tf_op jit(solution)/shard_map/ka,kc->ac/dot_general | solution.py:22
  211.9 0.0 copy-done.1
  211.9 0.0 copy-done.2
  211.9 3.3 %fusion.5 = bf16[1,640,2560]{2,1,0:T(8,128)(2,1)} fusion(f32[640,2560]{1,0:T(8,128)S(1)} %fusion.9, bf16[1,640,2560]{2,1,0:T(8,128)(2,1)S(1)} %copy-done.1, bf16[1,640,2560]{2,1,0:T(8,128)(2,1)S(1)} %copy-done.2), kind=kLoop, calls=%fused_computation.7 | loop fusion | flops 8192000 | bytes 16384000 | tf_op jit(solution)/shard_map/broadcast_in_dim | solution.py:23
  215.2 1.3 add_multiply_fusion
  216.5 2.4 %copy.10 = f32[640,320]{0,1:T(8,128)} copy(f32[640,320]{1,0:T(8,128)} %get-tuple-element.7) | data formatting | bytes 1638400
  218.9 1.2 copy.11
  (4 shorter events, 0.0 us)
Async XLA Ops:
  7.2 1.1 copy-start
  7.2 131.1 %copy-start.3 = (f32[640,320]{0,1:T(8,128)S(1)}, f32[640,320]{0,1:T(8,128)}, u32[]{:S(2)}) copy-start(f32[640,320]{0,1:T(8,128)} %param.7) | copy-start | bytes 2457604
  7.2 66.0 %all-reduce.3.cloned.1.call-start = ((), (), s32[]{:S(2)}) async-start(), calls=%async_computation.1 | async-start | bytes 327680 | tf_op jit(solution)/shard_map/psum | solution.py:13
  17.7 120.6 %reduce-scatter.2.cloned.1.call-start = ((), (), s32[]{:S(2)}) async-start(), calls=%async_computation.2 | async-start | bytes 819200 | tf_op jit(solution)/shard_map/reduce_scatter | solution.py:19
  112.5 80.7 %all-reduce.5.cloned.1.call-start = ((), (), s32[]{:S(2)}) async-start(), calls=%async_computation.3 | async-start | bytes 327680 | tf_op jit(solution)/shard_map/psum | solution.py:20
  193.3 18.6 %copy-start.1 = (bf16[1,640,2560]{2,1,0:T(8,128)(2,1)S(1)}, bf16[1,640,2560]{2,1,0:T(8,128)(2,1)}, u32[]{:S(2)}) copy-start(bf16[1,640,2560]{2,1,0:T(8,128)(2,1)} %param.5) | copy-start | bytes 9830404
  193.3 18.6 %copy-start.2 = (bf16[1,640,2560]{2,1,0:T(8,128)(2,1)S(1)}, bf16[1,640,2560]{2,1,0:T(8,128)(2,1)}, u32[]{:S(2)}) copy-start(bf16[1,640,2560]{2,1,0:T(8,128)(2,1)} %param.4) | copy-start | bytes 9830404
Sparse Core Ops, SparseCore 0:
  17.8 55.3 all-reduce.2
  112.7 25.5 reduce-scatter.1
  140.6 52.6 all-reduce.4
where the time goes:
time: 227 us
  waiting for transfers between devices  136 us (60%)
  blocking collectives  29.4 us (13%)
  matrix products  25.7 us (11%)
  other arithmetic  16.7 us (7%)
  between operations  13.8 us (6%)
  local copies, waits for them, and re-layouts  5.06 us (2%)
    psum x1, waiting for transfers between devices, body(): left = lax.psum(left_part, 'rep') / replicas  55.5 us
    psum x1, waiting for transfers between devices, body(): column_shares = lax.psum(column_shares, 'rep')  54.7 us
    reduce_scatter x1, waiting for transfers between devices, body(): lax.psum_scatter(right_part, 'mdl', scatter_dimension=1, tiled=True)  25.6 us
    psum x1, blocking collectives, body(): gram = lax.psum(gram, 'mdl')  16.2 us
    all_gather x1, blocking collectives, body(): right = lax.all_gather(column_shares, 'mdl', axis=1, tiled=True) / replicas  13.2 us
    dot_general x1, matrix products, body(): left_part = jnp.einsum('ac,ck->ka', merged, starts, precision=highest)  9.37 us
    dot_general x1, matrix products, body(): right_part = jnp.einsum('ac,ka->kc', merged, basis, precision=highest)  8.35 us
    another operation x3, other arithmetic, body(): lower = jnp.linalg.cholesky(gram)  6.52 us
  transfers between devices with their start and end apart: 3, of which 3 were waited for; matrix products, arithmetic and copies ran while one was open for 0% of the time, Pallas kernels for 0%

commit v1 on v0

v1 whole, which is shorter than its diff:
```python
import functools

import jax
import jax.numpy as jnp
from jax import lax
from jax.experimental import pallas as pl
from jax.experimental.pallas import tpu as pltpu
from jax.sharding import PartitionSpec as P

MESH = pl.DeviceIdType.MESH
highest = lax.Precision.HIGHEST
f32, bf16 = jnp.float32, jnp.bfloat16


def split3(x):
    hi = x.astype(bf16)
    rest = x - hi.astype(f32)
    mid = rest.astype(bf16)
    return hi, mid, (rest - mid.astype(f32)).astype(bf16)


def split2(x):
    hi = x.astype(bf16)
    return hi, (x - hi.astype(f32)).astype(bf16)


def when(cond, always):
    if always:
        return lambda f: f()
    return pl.when(cond)


def inverse(g, rank):
    rows = lax.broadcasted_iota(jnp.int32, (rank, rank), 0)
    cols = lax.broadcasted_iota(jnp.int32, (rank, rank), 1)
    for k in range(rank):
        row = g[k : k + 1, :]
        col = g[:, k : k + 1]
        scale = 1.0 / g[k : k + 1, k : k + 1]
        rowk, colk = rows == k, cols == k
        scaled = row * scale
        left = jnp.where(rowk[:, :1], 0.0, col)
        kept = jnp.where(colk, 0.0, g)
        fill = jnp.where(colk[:1, :], scale, scaled)
        g = jnp.where(rowk, fill, kept - left * fill)
    return g


def factors(
    nr, nm, shares, chunk, width,
    d_hbm, e_hbm, s_ref,
    y_ref, r_ref, own_ref,
    dv, ev, lpart, lrecv, lfull, gbuf, rpart, rrecv, rsum, zrecv, rfull,
    in_sem, ls_s, ls_r, lg_s, lg_r, g_s, g_r, rs_s, rs_r, zs_s, zs_r, zg_s, zg_r, rg_s, rg_r,
):
    rep, mdl = lax.axis_index("rep"), lax.axis_index("mdl")
    rank = s_ref.shape[1]
    per = rank // shares
    rows, channels = dv.shape
    cw = channels // nm
    chunks = rows // chunk
    everyone = shares == nr

    def rep_at(d):
        return lax.rem(rep + d + nr, nr)

    def mdl_at(d):
        return lax.rem(mdl + d + nm, nm)

    loads = []
    for i in range(chunks):
        span = pl.ds(i * chunk, chunk)
        pair = (
            pltpu.make_async_copy(d_hbm.at[span], dv.at[span], in_sem.at[0, i]),
            pltpu.make_async_copy(e_hbm.at[span], ev.at[span], in_sem.at[1, i]),
        )
        for c in pair:
            c.start()
        loads.append(pair)

    barrier = pltpu.get_barrier_semaphore()
    for d in range(1, nr):
        pl.semaphore_signal(barrier, inc=1, device_id=(rep_at(d), mdl), device_id_type=MESH)
    for d in range(1, nm):
        pl.semaphore_signal(barrier, inc=1, device_id=(rep, mdl_at(d)), device_id_type=MESH)

    s3 = jnp.concatenate(split3(s_ref[...].T), axis=0)
    nt = (((1,), (1,)), ((), ()))

    def fold(x):
        return x[:rank] + (x[rank : 2 * rank] + x[2 * rank :])

    for i in range(chunks):
        for c in loads[i]:
            c.wait()
        span = slice(i * chunk, (i + 1) * chunk)
        part = lax.dot_general(s3, dv[span, :], nt, preferred_element_type=f32)
        part += lax.dot_general(s3, ev[span, :], nt, preferred_element_type=f32)
        lpart[:, :, span] = fold(part).reshape(shares, per, chunk)

    pl.semaphore_wait(barrier, nr + nm - 2)

    def remote(src, dst, send, recv, to):
        return pltpu.make_async_remote_copy(
            src_ref=src, dst_ref=dst, send_sem=send, recv_sem=recv, device_id=to, device_id_type=MESH
        )

    def scatter(src, dst, send, recv):
        for d in range(1, nr):
            p = rep_at(d)

            @when(p < shares, everyone)
            def _():
                remote(src.at[p], dst.at[d], send.at[d], recv.at[d], (p, mdl)).start()

    def scatter_wait(src, dst, send, recv):
        for d in range(1, nr):

            @when(rep < shares, everyone)
            def _():
                remote(src.at[0], dst.at[d], send.at[d], recv.at[d], (rep, mdl)).wait_recv()

    def scatter_sent(src, dst, send, recv):
        for d in range(1, nr):
            p = rep_at(d)

            @when(p < shares, everyone)
            def _():
                remote(src.at[p], dst.at[d], send.at[d], recv.at[d], (p, mdl)).wait_send()

    def total(src, dst):
        t = src[rep]
        for d in range(1, nr):
            t = t + dst[d]
        return t / nr

    scatter(lpart, lrecv, ls_s, ls_r)
    scatter_wait(lpart, lrecv, ls_s, ls_r)

    @when(rep < shares, everyone)
    def _():
        lfull[rep] = total(lpart, lrecv)
        for d in range(1, nr):
            remote(lfull.at[rep], lfull.at[rep], lg_s.at[d], lg_r.at[d], (rep_at(d), mdl)).start()

    for d in range(1, nr):
        p = rep_at(-d)

        @when(p < shares, everyone)
        def _():
            remote(lfull.at[p], lfull.at[p], lg_s.at[d], lg_r.at[d], (rep, mdl)).wait_recv()

    left = lfull[...].reshape(rank, rows)

    gbuf[mdl] = lax.dot_general(left, left, nt, precision=highest, preferred_element_type=f32)
    for d in range(1, nm):
        remote(gbuf.at[mdl], gbuf.at[mdl], g_s.at[d], g_r.at[d], (rep, mdl_at(d))).start()

    l3 = jnp.concatenate(split3(left), axis=0)

    def product(cols):
        part = jnp.dot(l3, dv[:, cols], preferred_element_type=f32)
        part += jnp.dot(l3, ev[:, cols], preferred_element_type=f32)
        return fold(part).reshape(shares, per, cw)

    aligned = cw % 128 == 0
    if not aligned:
        for m in range(nm):
            rpart[m] = product(slice(m * cw, (m + 1) * cw))
    order = [lax.rem(rep + 1 + i, shares) for i in range(shares)]

    def to_mdl(d, i):
        j = order[i]
        return remote(
            rpart.at[mdl_at(d), j], rrecv.at[d, j], rs_s.at[d, i], rs_r.at[d, i], (rep, mdl_at(d))
        )

    for d in list(range(1, nm)) + [0]:
        if aligned:
            m = mdl_at(d)
            rpart[m] = product(pl.ds(pl.multiple_of(m * cw, 128), cw))
        if d > 0:
            for i in range(shares):
                to_mdl(d, i).start()

    for d in range(1, nm):
        p = mdl_at(-d)
        remote(gbuf.at[p], gbuf.at[p], g_s.at[d], g_r.at[d], (rep, mdl)).wait_recv()
    gram = gbuf[0]
    for m in range(1, nm):
        gram = gram + gbuf[m]
    y = lax.dot_general(
        left, inverse(gram, rank), (((0,), (0,)), ((), ())), precision=highest, preferred_element_type=f32
    )
    yh = y.astype(bf16).astype(f32)
    yl = y - yh
    y_ref[...] = jnp.concatenate([yh, yh, yl, yl], axis=1).astype(bf16)

    for i in range(shares):
        j = order[i]
        for d in range(1, nm):
            to_mdl(d, i).wait_recv()
        t = rpart[mdl, j]
        for d in range(1, nm):
            t = t + rrecv[d, j]
        rsum[j] = t
        for dr in range(1, nr):
            p = rep_at(dr)

            def send():
                remote(rsum.at[p], zrecv.at[dr], zs_s.at[dr], zs_r.at[dr], (p, mdl)).start()

            if everyone:
                if dr == i + 1:
                    send()
            elif i == shares - 1:
                pl.when(p < shares)(send)
    scatter_wait(rsum, zrecv, zs_s, zs_r)

    def forward(p, slot):
        for d in range(1, nm):
            remote(
                rfull.at[mdl, p], rfull.at[mdl, p], rg_s.at[d, slot], rg_r.at[d, slot], (rep, mdl_at(d))
            ).start()

    @when(rep < shares, everyone)
    def _():
        rfull[mdl, rep] = total(rsum, zrecv)
        for d in range(1, nr):
            remote(
                rfull.at[mdl, rep], rfull.at[mdl, rep], zg_s.at[d], zg_r.at[d], (rep_at(d), mdl)
            ).start()
        forward(rep, 0)

    for d in range(1, nr):
        p = rep_at(-d)

        @when(p < shares, everyone)
        def _():
            remote(rfull.at[mdl, p], rfull.at[mdl, p], zg_s.at[d], zg_r.at[d], (rep, mdl)).wait_recv()
            forward(p, d)

    for slot in range(nr):
        p = rep_at(-slot)

        @when(p < shares, everyone)
        def _():
            for d in range(1, nm):
                m = mdl_at(-d)
                remote(
                    rfull.at[m, p], rfull.at[m, p], rg_s.at[d, slot], rg_r.at[d, slot], (rep, mdl)
                ).wait_recv()

    for m in range(nm):
        hi, lo = split2(rfull[m].reshape(rank, cw))
        r_ref[:, m * cw : (m + 1) * cw] = jnp.concatenate([hi, lo, hi, lo], axis=0)
    for j in range(nr):

        @pl.when(rep == j)
        def _():
            own_ref[...] = r_ref[:, j * width : (j + 1) * width]

    scatter_sent(lpart, lrecv, ls_s, ls_r)
    scatter_sent(rsum, zrecv, zs_s, zs_r)

    @when(rep < shares, everyone)
    def _():
        for d in range(1, nr):
            remote(lfull.at[rep], lfull.at[rep], lg_s.at[d], lg_r.at[d], (rep_at(d), mdl)).wait_send()
            remote(
                rfull.at[mdl, rep], rfull.at[mdl, rep], zg_s.at[d], zg_r.at[d], (rep_at(d), mdl)
            ).wait_send()

    for d in range(1, nm):
        remote(gbuf.at[mdl], gbuf.at[mdl], g_s.at[d], g_r.at[d], (rep, mdl_at(d))).wait_send()
        for i in range(shares):
            to_mdl(d, i).wait_send()
        for slot in range(nr):
            p = rep_at(-slot)

            @when(p < shares, everyone)
            def _():
                remote(
                    rfull.at[mdl, p], rfull.at[mdl, p], rg_s.at[d, slot], rg_r.at[d, slot], (rep, mdl_at(d))
                ).wait_send()


def outputs(d_ref, e_ref, y_ref, r_ref, own_ref, m_ref, ne_ref, nm_ref, os_ref):
    approx = jnp.dot(y_ref[...], r_ref[...], preferred_element_type=f32)
    ne_ref[...] = ((d_ref[...].astype(f32) + e_ref[...].astype(f32)) - approx).astype(bf16)
    owned = jnp.dot(y_ref[...], own_ref[...], preferred_element_type=f32)
    new = 0.9 * m_ref[...] + owned
    nm_ref[...] = new
    os_ref[...] = 0.7 * (owned + 0.9 * new)


def body(nr, nm, deltas, errors, starts, momentum):
    deltas, errors = deltas[0], errors[0]
    rows, channels = deltas.shape
    rank = starts.shape[1]
    width = momentum.shape[1]
    shares = min(nr, max(rank // 8, 1))
    per = rank // shares
    cw = channels // nm
    chunk = 128 if rows % 128 == 0 else rows
    vmem = pl.BlockSpec(memory_space=pltpu.VMEM)
    hbm = pl.BlockSpec(memory_space=pl.ANY)
    dma = pltpu.SemaphoreType.DMA
    y, r, own = pl.pallas_call(
        functools.partial(factors, nr, nm, shares, chunk, width),
        name="factors",
        out_shape=(
            jax.ShapeDtypeStruct((rows, 4 * rank), bf16),
            jax.ShapeDtypeStruct((4 * rank, channels), bf16),
            jax.ShapeDtypeStruct((4 * rank, width), bf16),
        ),
        in_specs=[hbm, hbm, vmem],
        out_specs=(vmem, vmem, vmem),
        scratch_shapes=[
            pltpu.VMEM((rows, channels), bf16),
            pltpu.VMEM((rows, channels), bf16),
            pltpu.VMEM((shares, per, rows), f32),
            pltpu.VMEM((nr, per, rows), f32),
            pltpu.VMEM((shares, per, rows), f32),
            pltpu.VMEM((nm, rank, rank), f32),
            pltpu.VMEM((nm, shares, per, cw), f32),
            pltpu.VMEM((nm, shares, per, cw), f32),
            pltpu.VMEM((shares, per, cw), f32),
            pltpu.VMEM((nr, per, cw), f32),
            pltpu.VMEM((nm, shares, per, cw), f32),
            dma((2, rows // chunk)),
            dma((nr,)), dma((nr,)), dma((nr,)), dma((nr,)),
            dma((nm,)), dma((nm,)),
            dma((nm, shares)), dma((nm, shares)),
            dma((nr,)), dma((nr,)), dma((nr,)), dma((nr,)),
            dma((nm, nr)), dma((nm, nr)),
        ],
        compiler_params=pltpu.CompilerParams(
            collective_id=0, has_side_effects=True, vmem_limit_bytes=56 << 20
        ),
    )(deltas, errors, starts)

    def row_block(n):
        return pl.BlockSpec((chunk, n), lambda i: (i, 0))

    def whole(a):
        return pl.BlockSpec(a.shape, lambda i: (0, 0))

    new_errors, new_momentum, outer_step = pl.pallas_call(
        outputs,
        name="outputs",
        grid=(rows // chunk,),
        out_shape=(
            jax.ShapeDtypeStruct((rows, channels), bf16),
            jax.ShapeDtypeStruct((rows, width), f32),
            jax.ShapeDtypeStruct((rows, width), f32),
        ),
        in_specs=[
            row_block(channels), row_block(channels), row_block(4 * rank), whole(r), whole(own), row_block(width),
        ],
        out_specs=(row_block(channels), row_block(width), row_block(width)),
        compiler_params=pltpu.CompilerParams(vmem_limit_bytes=40 << 20),
    )(deltas, errors, y, r, own, momentum)
    return (new_errors[None], new_momentum, outer_step)


def solution(mesh):
    placed = (P("rep", "mdl", None), P("rep", "mdl", None), P(), P("mdl", "rep"))
    return jax.shard_map(
        functools.partial(body, mesh.shape["rep"], mesh.shape["mdl"]),
        mesh=mesh,
        in_specs=placed,
        out_specs=(P("rep", "mdl", None), P("mdl", "rep"), P("mdl", "rep")),
        check_vma=False,
    )
```

time: 227 us -> 71.2 us (0.31)
  waiting for transfers between devices: 136 us -> 0 us
  Pallas kernels: 0 us -> 56.2 us
  blocking collectives: 29.4 us -> 0 us
  matrix products: 25.7 us -> 0 us
  other arithmetic: 16.7 us -> 0 us
  between operations: 13.8 us -> 0.67 us
  local copies, waits for them, and re-layouts: 5.06 us -> 14 us
    psum x2 -> x0, waiting for transfers between devices: 110 us -> none  [the longest x1 55.5 us: body(): left = lax.psum(left_part, 'rep') / replicas]
    pallas_call x0 -> x2, Pallas kernels: none -> 56.2 us  [the longest x1 52.6 us: body(): pl.pallas_call(functools.partial(factors, nr, nm, shares, chunk, width),...]
    reduce_scatter x1 -> x0, waiting for transfers between devices: 25.6 us -> none  [body(): lax.psum_scatter(right_part, 'mdl', scatter_dimension=1, tiled=True)]
    dot_general x4 -> x0, matrix products: 24.5 us -> none  [the longest x1 9.37 us: body(): left_part = jnp.einsum('ac,ck->ka', merged, starts, precision=highest)]
    psum x1 -> x0, blocking collectives: 16.2 us -> none  [body(): gram = lax.psum(gram, 'mdl')]
    all_gather x1 -> x0, blocking collectives: 13.2 us -> none  [body(): right = lax.all_gather(column_shares, 'mdl', axis=1, tiled=True) / replicas]
    another operation x5 -> x0, other arithmetic: 12.1 us -> none  [the longest x3 6.52 us: body(): lower = jnp.linalg.cholesky(gram)]
    unnamed x11 -> x18, local copies, waits for them, and re-layouts: 4.99 us -> 14 us
  transfers between devices with their start and end apart: 3 -> 0, of which waited for: 3 -> 0; matrix products, arithmetic and copies ran while one was open for 0% -> 0% of each run, Pallas kernels for 0% -> 0%
where the time goes in v1:
time: 71.2 us; the launch traced here: 70.9 us
  Pallas kernels  56.2 us (79%)
  local copies, waits for them, and re-layouts  14 us (20%)
    pallas_call x1, Pallas kernels, body(): pl.pallas_call(functools.partial(factors, nr, nm, shares, chunk, width),...  52.6 us
    unnamed x18, local copies, waits for them, and re-layouts  14 us
    pallas_call x1, Pallas kernels, body(): pl.pallas_call(outputs, name='outputs', grid=(rows // chunk,), out_shape=...  3.54 us

profile of v1, /device:TPU:0, one launch (start us, length us, event | category | flops | bytes accessed | tf_op | source)
XLA Modules:
  0.0 70.9 jit_solution(12309394094719041612)
XLA Ops:
  0.6 1.5 %copy.8.m_ref = f32[640,320]{1,0:T(8,128)S(1)} copy(f32[640,320]{0,1:T(8,128)} %param.7) | data formatting | bytes 1638400 | tf_op args[3]
  2.1 2.6 %copy.7.s_ref = f32[2560,64]{1,0:T(8,128)} copy(f32[2560,64]{0,1:T(8,128)} %param.6) | data formatting | bytes 1310720 | tf_op args[2]
  4.7 0.0 copy-start
  4.7 0.0 copy-start.1
  4.7 52.6 %factors.1 = (bf16[640,256]{1,0:T(8,128)(2,1)}, bf16[256,2560]{1,0:T(8,128)(2,1)}, bf16[256,320]{1,0:T(8,128)(2,1)}) custom-call(bf16[640,2560]{1,0:T(8,128)(2,1)} %bitcast.3, bf16[640,2560]{1,0:T(8,128)(2,1)} %bitcast.5, f32[2560,64]{1,0:T(8,128)} %copy.7.s_ref), custom_call_target="tpu_custom_call" | custom-call | tf_op jit(solution)/shard_map/factors/pallas_call | solution.py:309
  57.3 0.0 copy-done
  57.3 0.0 copy-done.1
  57.3 0.0 copy-start.2
  57.3 1.3 %copy-done.2 = bf16[256,2560]{1,0:T(8,128)(2,1)S(1)} copy-done((bf16[256,2560]{1,0:T(8,128)(2,1)S(1)}, bf16[256,2560]{1,0:T(8,128)(2,1)}, u32[]{:S(2)}) %copy-start.2) | copy-done | bytes 1310744
  58.7 0.0 copy-start.5
  58.7 1.0 %copy-done.5 = bf16[640,256]{1,0:T(8,128)(2,1)S(1)} copy-done((bf16[640,256]{1,0:T(8,128)(2,1)S(1)}, bf16[640,256]{1,0:T(8,128)(2,1)}, u32[]{:S(2)}) %copy-start.5) | copy-done | bytes 327704
  59.6 0.0 copy-start.6
  59.6 0.9 %copy-done.6 = bf16[256,320]{1,0:T(8,128)(2,1)S(1)} copy-done((bf16[256,320]{1,0:T(8,128)(2,1)S(1)}, bf16[256,320]{1,0:T(8,128)(2,1)}, u32[]{:S(2)}) %copy-start.6) | copy-done | bytes 163864
  60.6 3.5 %outputs.1 = (bf16[640,2560]{1,0:T(8,128)(2,1)}, f32[640,320]{1,0:T(8,128)S(1)}, f32[640,320]{1,0:T(8,128)S(1)}) custom-call(bf16[640,2560]{1,0:T(8,128)(2,1)S(1)} %bitcast.4, bf16[640,2560]{1,0:T(8,128)(2,1)S(1)} %bitcast.6, bf16[640,256]{1,0:T(8,128)(2,1)S(1)} %copy-done.5, bf16[256,2560]{1,0:T(8,128)(2,1)S(1)} %copy-done.2, ...), custom_call_target="tpu_custom_call" | custom-call | tf_op jit(solution)/shard_map/outputs/pallas_call | solution.py:349
  64.1 0.0 copy-start.3
  64.1 0.9 %copy-done.3 = f32[640,320]{1,0:T(8,128)} copy-done((f32[640,320]{1,0:T(8,128)}, f32[640,320]{1,0:T(8,128)S(1)}, u32[]{:S(2)}) %copy-start.3) | copy-done | bytes 819224
  65.0 0.0 copy-start.4
  65.0 1.0 %copy-done.4 = f32[640,320]{1,0:T(8,128)} copy-done((f32[640,320]{1,0:T(8,128)}, f32[640,320]{1,0:T(8,128)S(1)}, u32[]{:S(2)}) %copy-start.4) | copy-done | bytes 819224
  66.0 2.4 %copy.9 = f32[640,320]{0,1:T(8,128)} copy(f32[640,320]{1,0:T(8,128)} %copy-done.4) | data formatting | bytes 1638400
  68.5 2.4 %copy.10 = f32[640,320]{0,1:T(8,128)} copy(f32[640,320]{1,0:T(8,128)} %copy-done.3) | data formatting | bytes 1638400
Async XLA Ops:
  4.7 52.7 %copy-start = (bf16[1,640,2560]{2,1,0:T(8,128)(2,1)S(1)}, bf16[1,640,2560]{2,1,0:T(8,128)(2,1)}, u32[]{:S(2)}) copy-start(bf16[1,640,2560]{2,1,0:T(8,128)(2,1)} %param.4) | copy-start | bytes 9830404
  4.7 52.7 %copy-start.1 = (bf16[1,640,2560]{2,1,0:T(8,128)(2,1)S(1)}, bf16[1,640,2560]{2,1,0:T(8,128)(2,1)}, u32[]{:S(2)}) copy-start(bf16[1,640,2560]{2,1,0:T(8,128)(2,1)} %param.5) | copy-start | bytes 9830404
  57.3 1.3 %copy-start.2 = (bf16[256,2560]{1,0:T(8,128)(2,1)S(1)}, bf16[256,2560]{1,0:T(8,128)(2,1)}, u32[]{:S(2)}) copy-start(bf16[256,2560]{1,0:T(8,128)(2,1)} %get-tuple-element.10.r_ref) | copy-start | bytes 3932164
  58.7 1.0 %copy-start.5 = (bf16[640,256]{1,0:T(8,128)(2,1)S(1)}, bf16[640,256]{1,0:T(8,128)(2,1)}, u32[]{:S(2)}) copy-start(bf16[640,256]{1,0:T(8,128)(2,1)} %get-tuple-element.9.y_ref) | copy-start | bytes 983044
  59.6 0.9 %copy-start.6 = (bf16[256,320]{1,0:T(8,128)(2,1)S(1)}, bf16[256,320]{1,0:T(8,128)(2,1)}, u32[]{:S(2)}) copy-start(bf16[256,320]{1,0:T(8,128)(2,1)} %get-tuple-element.11.own_ref) | copy-start | bytes 491524
  64.1 0.9 %copy-start.3 = (f32[640,320]{1,0:T(8,128)}, f32[640,320]{1,0:T(8,128)S(1)}, u32[]{:S(2)}) copy-start(f32[640,320]{1,0:T(8,128)S(1)} %get-tuple-element.17) | copy-start | bytes 2457604
  65.0 1.0 %copy-start.4 = (f32[640,320]{1,0:T(8,128)}, f32[640,320]{1,0:T(8,128)S(1)}, u32[]{:S(2)}) copy-start(f32[640,320]{1,0:T(8,128)S(1)} %get-tuple-element.16) | copy-start | bytes 2457604

commit v2 on v0

v2 whole, which is shorter than its diff:
```python
import functools

import jax
import jax.numpy as jnp
from jax import lax
from jax.experimental import pallas as pl
from jax.experimental.pallas import tpu as pltpu
from jax.sharding import PartitionSpec as P

MESH = pl.DeviceIdType.MESH
highest = lax.Precision.HIGHEST
f32, bf16 = jnp.float32, jnp.bfloat16


def split3(x):
    hi = x.astype(bf16)
    rest = x - hi.astype(f32)
    mid = rest.astype(bf16)
    return hi, mid, (rest - mid.astype(f32)).astype(bf16)


def split2(x):
    hi = x.astype(bf16)
    return hi, (x - hi.astype(f32)).astype(bf16)


def when(cond, always):
    if always:
        return lambda f: f()
    return pl.when(cond)


def sweep(g, rank, first, last):
    rows = lax.broadcasted_iota(jnp.int32, (rank, rank), 0)
    cols = lax.broadcasted_iota(jnp.int32, (rank, rank), 1)
    for k in range(first, last):
        row = g[k : k + 1, :]
        col = g[:, k : k + 1]
        scale = 1.0 / g[k : k + 1, k : k + 1]
        rowk, colk = rows == k, cols == k
        left = jnp.where(rowk[:, :1], 0.0, col)
        kept = jnp.where(colk, 0.0, g)
        fill = jnp.where(colk[:1, :], scale, row * scale)
        g = jnp.where(rowk, fill, kept - left * fill)
    return g


def factors(
    nr, nm, shares, chunk, width,
    d_hbm, e_hbm, s_ref,
    fac_ref, dv, ev,
    lpart, lpair, lsum, lrecv, lfull, gbuf, rpart, rpair, rsum, rrecv, zsum, zrecv, rfull,
    in_sem, lp_s, lp_r, ls_s, ls_r, lg_s, lg_r, lf_s, lf_r, g_s, g_r,
    rp_s, rp_r, rs_s, rs_r, zs_s, zs_r, zg_s, zg_r, rg_s, rg_r, rf_s, rf_r,
):
    rep, mdl = lax.axis_index("rep"), lax.axis_index("mdl")
    z, core = lax.div(rep, 2), lax.rem(rep, 2)
    other = 1 - core
    nz = nr // 2
    rank = s_ref.shape[0]
    per = rank // (2 * shares)
    rows, channels = dv.shape
    cw = channels // nm
    chunks = rows // chunk
    everyone = shares == nz
    owner = when(z < shares, everyone)
    partner = (2 * z + other, mdl)

    def z_at(d):
        return lax.rem(z + d + nz, nz)

    def mdl_at(d):
        return lax.rem(mdl + d + nm, nm)

    def z_peer(d):
        return (2 * z_at(d) + core, mdl)

    def mdl_peer(d):
        return (rep, mdl_at(d))

    def remote(src, dst, send, recv, to):
        return pltpu.make_async_remote_copy(
            src_ref=src, dst_ref=dst, send_sem=send, recv_sem=recv, device_id=to, device_id_type=MESH
        )

    sent = []

    def start(copy, guard=None):
        if guard is None:
            copy().start()
            sent.append(lambda: copy().wait_send())
        else:
            guard(lambda: copy().start())
            sent.append(lambda: guard(lambda: copy().wait_send()))

    loads = []
    for i in range(chunks):
        span = pl.ds(i * chunk, chunk)
        pair = (
            pltpu.make_async_copy(d_hbm.at[span], dv.at[span], in_sem.at[0, i]),
            pltpu.make_async_copy(e_hbm.at[span], ev.at[span], in_sem.at[1, i]),
        )
        for c in pair:
            c.start()
        loads.append(pair)

    barrier = pltpu.get_barrier_semaphore()
    friends = [partner] + [z_peer(d) for d in range(1, nz)] + [mdl_peer(d) for d in range(1, nm)]
    for f in friends:
        pl.semaphore_signal(barrier, inc=1, device_id=f, device_id_type=MESH)

    s3 = jnp.concatenate(split3(s_ref[...]), axis=0)
    nt = (((1,), (1,)), ((), ()))

    def fold(x):
        return x[:rank] + (x[rank : 2 * rank] + x[2 * rank :])

    def lp(i):
        span = pl.ds(i * chunk, chunk)
        return remote(
            lpart.at[other, :, :, span], lpair.at[:, :, span], lp_s.at[i], lp_r.at[i], partner
        )

    def ls(d, i):
        span = pl.ds(i * chunk, chunk)
        return remote(
            lsum.at[z_at(d), :, span], lrecv.at[d, :, span], ls_s.at[d, i], ls_r.at[d, i], z_peer(d)
        )

    def left_pass(i):
        lp(i).wait_recv()
        span = slice(i * chunk, (i + 1) * chunk)
        lsum[:, :, span] = lpart[core, :, :, span] + lpair[:, :, span]
        for d in range(1, nz):
            start(functools.partial(ls, d, i), None if everyone else pl.when(z_at(d) < shares))

    for i in range(chunks):
        for c in loads[i]:
            c.wait()
        span = slice(i * chunk, (i + 1) * chunk)
        part = lax.dot_general(s3, dv[span, :], nt, preferred_element_type=f32)
        part += lax.dot_general(s3, ev[span, :], nt, preferred_element_type=f32)
        lpart[:, :, :, span] = fold(part).reshape(2, shares, per, chunk)
        if i == 0:
            pl.semaphore_wait(barrier, len(friends))
        start(functools.partial(lp, i))
        if i > 0:
            left_pass(i - 1)
    left_pass(chunks - 1)

    def lg(d):
        return remote(lfull.at[core, z], lfull.at[core, z], lg_s.at[d], lg_r.at[d], z_peer(d))

    def lf(d):
        p = z_at(-d)
        return remote(lfull.at[core, p], lfull.at[core, p], lf_s.at[d], lf_r.at[d], partner)

    def lf_in(d):
        p = z_at(-d)
        return remote(lfull.at[other, p], lfull.at[other, p], lf_s.at[d], lf_r.at[d], partner)

    @owner
    def _():
        for i in range(chunks):
            for d in range(1, nz):
                ls(d, i).wait_recv()
        t = lsum[z]
        for d in range(1, nz):
            t = t + lrecv[d]
        lfull[core, z] = t / nr

    for d in range(1, nz):
        start(functools.partial(lg, d), None if everyone else pl.when(z < shares))
    start(functools.partial(lf, 0), None if everyone else pl.when(z < shares))
    for d in range(1, nz):
        guard = None if everyone else pl.when(z_at(-d) < shares)

        def lg_in(d=d):
            p = z_at(-d)
            remote(lfull.at[core, p], lfull.at[core, p], lg_s.at[d], lg_r.at[d], partner).wait_recv()

        lg_in() if guard is None else guard(lg_in)
        start(functools.partial(lf, d), guard)
    for d in range(nz):
        when(z_at(-d) < shares, everyone)(lambda: lf_in(d).wait_recv())

    left = lfull[...].reshape(rank, rows)

    def gr(d):
        return remote(gbuf.at[mdl], gbuf.at[mdl], g_s.at[d], g_r.at[d], mdl_peer(d))

    gbuf[mdl] = lax.dot_general(left, left, nt, precision=highest, preferred_element_type=f32)
    for d in range(1, nm):
        start(functools.partial(gr, d))

    l3 = jnp.concatenate(split3(left), axis=0)

    def product(cols):
        part = jnp.dot(l3, dv[:, cols], preferred_element_type=f32)
        part += jnp.dot(l3, ev[:, cols], preferred_element_type=f32)
        return fold(part).reshape(2, shares, per, cw)

    aligned = cw % 128 == 0
    if not aligned:
        for m in range(nm):
            rpart[m] = product(slice(m * cw, (m + 1) * cw))
    order = [lax.rem(z + 1 + i, shares) for i in range(shares)]

    def rp(d):
        m = mdl_at(d)
        return remote(rpart.at[m, other], rpair.at[d], rp_s.at[d], rp_r.at[d], partner)

    def rs(d, i):
        j = order[i]
        return remote(rsum.at[d, j], rrecv.at[d, j], rs_s.at[d, i], rs_r.at[d, i], mdl_peer(d))

    def pair_pass(d):
        rp(d).wait_recv()
        rsum[d] = rpart[mdl_at(d), core] + rpair[d]
        if d > 0:
            for i in range(shares):
                start(functools.partial(rs, d, i))

    turns = list(range(1, nm)) + [0]
    for n, d in enumerate(turns):
        if aligned:
            m = mdl_at(d)
            rpart[m] = product(pl.ds(pl.multiple_of(m * cw, 128), cw))
        start(functools.partial(rp, d))
        if n > 0:
            pair_pass(turns[n - 1])
    pair_pass(turns[-1])

    for d in range(1, nm):
        p = mdl_at(-d)
        remote(gbuf.at[p], gbuf.at[p], g_s.at[d], g_r.at[d], partner).wait_recv()
    gram = gbuf[0]
    for m in range(1, nm):
        gram = gram + gbuf[m]
    cuts = [0, (rank * 20) // 64, (rank * 42) // 64, rank]
    gram = sweep(gram, rank, cuts[0], cuts[1])

    def zs(d):
        return remote(zsum.at[z_at(d)], zrecv.at[d], zs_s.at[d], zs_r.at[d], z_peer(d))

    for i in range(shares):
        j = order[i]
        for d in range(1, nm):
            rs(d, i).wait_recv()
        t = rsum[0, j]
        for d in range(1, nm):
            t = t + rrecv[d, j]
        zsum[j] = t
        if everyone and i + 1 < nz:
            start(functools.partial(zs, i + 1))
    if not everyone:
        for d in range(1, nz):
            start(functools.partial(zs, d), pl.when(z_at(d) < shares))

    gram = sweep(gram, rank, cuts[1], cuts[2])

    def zg(d):
        return remote(rfull.at[mdl, core, z], rfull.at[mdl, core, z], zg_s.at[d], zg_r.at[d], z_peer(d))

    def rg(d, slot):
        p = z_at(-slot)
        return remote(
            rfull.at[mdl, core, p], rfull.at[mdl, core, p], rg_s.at[d, slot], rg_r.at[d, slot], mdl_peer(d)
        )

    def rf(d, slot):
        m, p = mdl_at(-d), z_at(-slot)
        return remote(
            rfull.at[m, core, p], rfull.at[m, core, p], rf_s.at[d, slot], rf_r.at[d, slot], partner
        )

    def rf_in(d, slot):
        m, p = mdl_at(-d), z_at(-slot)
        return remote(
            rfull.at[m, other, p], rfull.at[m, other, p], rf_s.at[d, slot], rf_r.at[d, slot], partner
        )

    @owner
    def _():
        for d in range(1, nz):
            zs(d).wait_recv()
        t = zsum[z]
        for d in range(1, nz):
            t = t + zrecv[d]
        rfull[mdl, core, z] = t / nr

    def spread(slot, guard):
        for d in range(1, nm):
            start(functools.partial(rg, d, slot), guard)
        start(functools.partial(rf, 0, slot), guard)

    mine = None if everyone else pl.when(z < shares)
    for d in range(1, nz):
        start(functools.partial(zg, d), mine)
    spread(0, mine)

    gram = sweep(gram, rank, cuts[2], cuts[3])

    for slot in range(1, nz):
        guard = None if everyone else pl.when(z_at(-slot) < shares)

        def zg_in(slot=slot):
            p = z_at(-slot)
            remote(
                rfull.at[mdl, core, p], rfull.at[mdl, core, p], zg_s.at[slot], zg_r.at[slot], partner
            ).wait_recv()

        zg_in() if guard is None else guard(zg_in)
        spread(slot, guard)

    fac_ref[:, channels : channels + rows] = jnp.dot(gram, left, precision=highest, preferred_element_type=f32)

    for slot in range(nz):
        guard = None if everyone else pl.when(z_at(-slot) < shares)
        for d in range(1, nm):

            def rg_in(d=d, slot=slot):
                m, p = mdl_at(-d), z_at(-slot)
                remote(
                    rfull.at[m, core, p], rfull.at[m, core, p], rg_s.at[d, slot], rg_r.at[d, slot], partner
                ).wait_recv()

            rg_in() if guard is None else guard(rg_in)
            start(functools.partial(rf, d, slot), guard)
    for slot in range(nz):
        for d in range(nm):
            when(z_at(-slot) < shares, everyone)(lambda: rf_in(d, slot).wait_recv())

    for m in range(nm):
        fac_ref[:, m * cw : (m + 1) * cw] = rfull[m].reshape(rank, cw)
    for j in range(nr):

        @pl.when(rep == j)
        def _():
            fac_ref[:, channels + rows :] = fac_ref[:, j * width : (j + 1) * width]

    for f in sent:
        f()


def outputs(chunks, d_ref, e_ref, f_ref, m_ref, ne_ref, nm_ref, os_ref, right, own):
    step = pl.program_id(0)
    chunk, channels = d_ref.shape
    rows = chunk * chunks

    @pl.when(step == 0)
    def _():
        hi, lo = split2(f_ref[:, :channels])
        right[...] = jnp.concatenate([hi, lo, hi, lo], axis=0)
        hi, lo = split2(f_ref[:, channels + rows :])
        own[...] = jnp.concatenate([hi, lo, hi, lo], axis=0)

    start = channels if chunks == 1 else pl.multiple_of(channels + step * chunk, 128)
    hi, lo = split2(f_ref[:, pl.ds(start, chunk)])
    y = jnp.concatenate([hi, hi, lo, lo], axis=0)
    tn = (((0,), (0,)), ((), ()))
    approx = lax.dot_general(y, right[...], tn, preferred_element_type=f32)
    ne_ref[...] = ((d_ref[...].astype(f32) + e_ref[...].astype(f32)) - approx).astype(bf16)
    owned = lax.dot_general(own[...], y, tn, preferred_element_type=f32)
    new = 0.9 * m_ref[...] + owned
    nm_ref[...] = new
    os_ref[...] = 0.7 * (owned + 0.9 * new)


def body(nr, nm, deltas, errors, starts, momentum):
    deltas, errors, starts, momentum = deltas[0], errors[0], starts.T, momentum.T
    rows, channels = deltas.shape
    rank = starts.shape[0]
    width = momentum.shape[0]
    nz = nr // 2
    shares = min(nz, max(rank // 16, 1))
    per = rank // (2 * shares)
    cw = channels // nm
    chunk = 128 if rows % 128 == 0 else rows
    chunks = rows // chunk
    vmem = pl.BlockSpec(memory_space=pltpu.VMEM)
    hbm = pl.BlockSpec(memory_space=pltpu.HBM)
    dma = pltpu.SemaphoreType.DMA
    fac, deltas, errors = pl.pallas_call(
        functools.partial(factors, nr, nm, shares, chunk, width),
        name="factors",
        out_shape=(
            jax.ShapeDtypeStruct((rank, channels + rows + width), f32),
            jax.ShapeDtypeStruct((rows, channels), bf16),
            jax.ShapeDtypeStruct((rows, channels), bf16),
        ),
        in_specs=[hbm, hbm, vmem],
        out_specs=(vmem, vmem, vmem),
        scratch_shapes=[
            pltpu.VMEM((2, shares, per, rows), f32),
            pltpu.VMEM((shares, per, rows), f32),
            pltpu.VMEM((shares, per, rows), f32),
            pltpu.VMEM((nz, per, rows), f32),
            pltpu.VMEM((2, shares, per, rows), f32),
            pltpu.VMEM((nm, rank, rank), f32),
            pltpu.VMEM((nm, 2, shares, per, cw), f32),
            pltpu.VMEM((nm, shares, per, cw), f32),
            pltpu.VMEM((nm, shares, per, cw), f32),
            pltpu.VMEM((nm, shares, per, cw), f32),
            pltpu.VMEM((shares, per, cw), f32),
            pltpu.VMEM((nz, per, cw), f32),
            pltpu.VMEM((nm, 2, shares, per, cw), f32),
            dma((2, chunks)),
            dma((chunks,)), dma((chunks,)), dma((nz, chunks)), dma((nz, chunks)),
            dma((nz,)), dma((nz,)), dma((nz,)), dma((nz,)),
            dma((nm,)), dma((nm,)),
            dma((nm,)), dma((nm,)), dma((nm, shares)), dma((nm, shares)),
            dma((nz,)), dma((nz,)), dma((nz,)), dma((nz,)),
            dma((nm, nz)), dma((nm, nz)), dma((nm, nz)), dma((nm, nz)),
        ],
        compiler_params=pltpu.CompilerParams(
            collective_id=0, has_side_effects=True, vmem_limit_bytes=46 << 20
        ),
    )(deltas, errors, starts)

    def row_block(n):
        return pl.BlockSpec((chunk, n), lambda i: (i, 0))

    def column_block(n):
        return pl.BlockSpec((n, chunk), lambda i: (0, i))

    new_errors, new_momentum, outer_step = pl.pallas_call(
        functools.partial(outputs, chunks),
        name="outputs",
        grid=(rows // chunk,),
        out_shape=(
            jax.ShapeDtypeStruct((rows, channels), bf16),
            jax.ShapeDtypeStruct((width, rows), f32),
            jax.ShapeDtypeStruct((width, rows), f32),
        ),
        in_specs=[
            row_block(channels), row_block(channels), pl.BlockSpec(fac.shape, lambda i: (0, 0)), column_block(width),
        ],
        out_specs=(row_block(channels), column_block(width), column_block(width)),
        scratch_shapes=[pltpu.VMEM((4 * rank, channels), bf16), pltpu.VMEM((4 * rank, width), bf16)],
        compiler_params=pltpu.CompilerParams(vmem_limit_bytes=40 << 20),
    )(deltas, errors, fac, momentum)
    return (new_errors[None], new_momentum.T, outer_step.T)


def solution(mesh):
    placed = (P("rep", "mdl", None), P("rep", "mdl", None), P(), P("mdl", "rep"))
    return jax.shard_map(
        functools.partial(body, mesh.shape["rep"], mesh.shape["mdl"]),
        mesh=mesh,
        in_specs=placed,
        out_specs=(P("rep", "mdl", None), P("mdl", "rep"), P("mdl", "rep")),
        check_vma=False,
    )
```

time: 227 us -> 49.6 us (0.22)
  waiting for transfers between devices: 136 us -> 0 us
  Pallas kernels: 0 us -> 47.6 us
  blocking collectives: 29.4 us -> 0 us
  matrix products: 25.7 us -> 0 us
  other arithmetic: 16.7 us -> 0 us
  between operations: 13.8 us -> 0.66 us
  local copies, waits for them, and re-layouts: 5.06 us -> 1.08 us
    psum x2 -> x0, waiting for transfers between devices: 110 us -> none  [the longest x1 55.5 us: body(): left = lax.psum(left_part, 'rep') / replicas]
    pallas_call x0 -> x2, Pallas kernels: none -> 47.6 us  [the longest x1 43.4 us: body(): pl.pallas_call(functools.partial(factors, nr, nm, shares, chunk, width),...]
    reduce_scatter x1 -> x0, waiting for transfers between devices: 25.6 us -> none  [body(): lax.psum_scatter(right_part, 'mdl', scatter_dimension=1, tiled=True)]
    dot_general x4 -> x0, matrix products: 24.5 us -> none  [the longest x1 9.37 us: body(): left_part = jnp.einsum('ac,ck->ka', merged, starts, precision=highest)]
    psum x1 -> x0, blocking collectives: 16.2 us -> none  [body(): gram = lax.psum(gram, 'mdl')]
    all_gather x1 -> x0, blocking collectives: 13.2 us -> none  [body(): right = lax.all_gather(column_shares, 'mdl', axis=1, tiled=True) / replicas]
    another operation x5 -> x0, other arithmetic: 12.1 us -> none  [the longest x3 6.52 us: body(): lower = jnp.linalg.cholesky(gram)]
    unnamed x11 -> x4, local copies, waits for them, and re-layouts: 4.99 us -> 1.08 us
  transfers between devices with their start and end apart: 3 -> 0, of which waited for: 3 -> 0; matrix products, arithmetic and copies ran while one was open for 0% -> 0% of each run, Pallas kernels for 0% -> 0%
where the time goes in v2:
time: 49.6 us; the launch traced here: 49.3 us
  Pallas kernels  47.6 us (96%)
  local copies, waits for them, and re-layouts  1.08 us (2%)
  between operations  0.66 us (1%)
    pallas_call x1, Pallas kernels, body(): pl.pallas_call(functools.partial(factors, nr, nm, shares, chunk, width),...  43.4 us
    pallas_call x1, Pallas kernels, body(): pl.pallas_call(functools.partial(outputs, chunks), name='outputs', grid=(...  4.17 us
    unnamed x4, local copies, waits for them, and re-layouts  1.08 us

profile of v2, /device:TPU:0, one launch (start us, length us, event | category | flops | bytes accessed | tf_op | source)
XLA Modules:
  0.0 49.3 jit_solution(15270771041560063924)
XLA Ops:
  0.6 0.0 copy-start.1
  0.6 1.1 %copy-done.1 = f32[2560,64]{0,1:T(8,128)S(1)} copy-done((f32[2560,64]{0,1:T(8,128)S(1)}, f32[2560,64]{0,1:T(8,128)}, u32[]{:S(2)}) %copy-start.1) | copy-done | bytes 655384
  1.7 0.0 copy-start
  1.7 43.4 %factors.1 = (f32[64,3520]{1,0:T(8,128)S(1)}, bf16[640,2560]{1,0:T(8,128)(2,1)S(1)}, bf16[640,2560]{1,0:T(8,128)(2,1)S(1)}) custom-call(bf16[640,2560]{1,0:T(8,128)(2,1)} %bitcast.9, bf16[640,2560]{1,0:T(8,128)(2,1)} %bitcast.10, f32[64,2560]{1,0:T(8,128)S(1)} %bitcast.8), custom_call_target="tpu_custom_call" | custom-call | tf_op jit(solution)/shard_map/factors/pallas_call | solution.py:384
  45.1 0.0 copy-done
  45.1 4.2 %outputs.1 = (bf16[640,2560]{1,0:T(8,128)(2,1)}, f32[320,640]{1,0:T(8,128)}, f32[320,640]{1,0:T(8,128)}) custom-call(bf16[640,2560]{1,0:T(8,128)(2,1)S(1)} %get-tuple-element.9.d_ref, bf16[640,2560]{1,0:T(8,128)(2,1)S(1)} %get-tuple-element.10.e_ref, f32[64,3520]{1,0:T(8,128)S(1)} %get-tuple-element.11.f_ref, f32[320,640]{1,0:T(8,128)S(1)} %bitcast.7), custom_call_target="tpu_custom_call" | custom-call | tf_op jit(solution)/shard_map/outputs/pallas_call | solution.py:427
Async XLA Ops:
  0.6 1.1 %copy-start.1 = (f32[2560,64]{0,1:T(8,128)S(1)}, f32[2560,64]{0,1:T(8,128)}, u32[]{:S(2)}) copy-start(f32[2560,64]{0,1:T(8,128)} %param.6) | copy-start | bytes 1966084
  1.7 43.4 %copy-start = (f32[640,320]{0,1:T(8,128)S(1)}, f32[640,320]{0,1:T(8,128)}, u32[]{:S(2)}) copy-start(f32[640,320]{0,1:T(8,128)} %param.7) | copy-start | bytes 2457604
